TPU v7x, 128 devices: a whole 4x4x4 slice. The times are simulated.
128 devices in a mesh: row: 8 (over z, core), col: 16 (over y, x).
Axes of the slice: x: 4, y: 4, z: 4, core: 2. Of those that a mesh axis runs over, the one named last changes fastest.
Arguments:
- snapshots: bfloat16 [4096, 32768], P('row', 'col'), may hold values from -14 to 14
- neighbours: int32 [4096, 128], P('row'), may hold values from 0 to 4095, all different within a row
- start_basis: float32 [32, 4096], replicated, may hold values from -6 to 6
Outputs:
- basis: float32 [32, 4096], P(None, 'row')
- rayleigh: float32 [32, 32], replicated
Inputs may be any that keep to these rules, and one draw needn't show every extreme that they name: `neighbours`: each row names 128 different snapshots.
All inputs are finite; a program needn't handle non-finite values.
Results may differ from a plain program's by a relative error of at most 0.00145.
Values may be sent and summed in bfloat16 or wider, within the bound.
No kernel may reach another device: no remote copies, remote signals or barrier semaphores. Data moves between devices by JAX's collectives and lax.ppermute only.
A program may use at most 128 MiB of HBM per device.

v0:
```python
import math
import jax
import jax.numpy as jnp
from jax import lax
from jax.sharding import PartitionSpec as P

FEATURES = 32768
LAGS = 64
ITERS = 2


def global_sum(value):
    return lax.psum(value, ("row", "col"))


def collect(columns):
    return lax.all_gather(columns, ("row", "col"), axis=1, tiled=True)


def shards(snapshots, neighbours, start_basis):
    row_count = lax.axis_size("row")
    col_count = lax.axis_size("col")
    row_at = lax.axis_index("row")
    col_at = lax.axis_index("col")
    lag_count = LAGS
    whole = lax.all_gather(snapshots, "row", axis=0, tiled=True)
    snap_count = whole.shape[0]
    feat_width = whole.shape[1]
    col_block = snap_count // col_count
    row_block = snapshots.shape[0]
    squares = jnp.sum(jnp.square(whole.astype(jnp.float32)), axis=1)
    padded_rows = jnp.concatenate([jnp.zeros((lag_count, feat_width), whole.dtype), whole], 0)
    padded_norms = jnp.concatenate([jnp.zeros((lag_count,), jnp.float32), squares], 0)
    row_start = row_at * row_block
    ext_rows = lax.dynamic_slice_in_dim(padded_rows, row_start, row_block + lag_count, 0)
    ext_norms = lax.dynamic_slice_in_dim(padded_norms, row_start, row_block + lag_count, 0)
    row_times = row_start - lag_count + jnp.arange(row_block + lag_count, dtype=jnp.int32)
    span = col_block + lag_count
    blocks = whole.reshape(col_count, col_block, feat_width)
    earlier = jnp.concatenate(
        [jnp.zeros((1, lag_count, feat_width), whole.dtype), blocks[:-1, col_block - lag_count :]],
        0,
    )
    source_rows = jnp.concatenate([earlier, blocks], 1).reshape(col_count * span, feat_width)
    norm_blocks = squares.reshape(col_count, col_block)
    norm_earlier = jnp.concatenate(
        [jnp.zeros((1, lag_count), jnp.float32), norm_blocks[:-1, col_block - lag_count :]], 0
    )
    source_norms = jnp.concatenate([norm_earlier, norm_blocks], 1).reshape(col_count * span)
    virtual = jnp.arange(span * lax.axis_size("col"), dtype=jnp.int32)
    times = virtual // span * col_block + virtual % span - lag_count
    inner = lax.dot_general(
        source_rows, ext_rows, (((1,), (1,)), ((), ())), preferred_element_type=jnp.float32
    )
    term = source_norms[:, None] + ext_norms[None, :] - 2.0 * inner
    keep = (times >= 0)[:, None] & (row_times >= 0)[None, :]
    tile = lax.psum_scatter(
        jnp.where(keep, term, 0.0).astype(jnp.bfloat16), "col", scatter_dimension=0, tiled=True
    ).astype(jnp.float32)
    window = 1
    while window < lag_count:
        tile = tile[window:, window:] + tile[:-window, :-window]
        window = window * 2
    lagged = tile[1:, 1:]
    step_rows = math.gcd(row_block, 16)
    block_count = row_block // step_rows
    slot_count = neighbours.shape[1]
    offset = neighbours - col_at * col_block
    inside = (offset >= 0) & (offset < col_block)
    tile_positions = jnp.arange(col_block, dtype=jnp.int32)

    def pick_block(pair):
        offs, lag_rows = pair
        match = offs[:, :, None] == tile_positions[None, None, :]
        return jnp.sum(jnp.where(match, lag_rows[:, None, :], 0.0), axis=2)

    chosen = lax.map(
        pick_block,
        (
            offset.reshape(block_count, step_rows, slot_count),
            lagged.T.reshape(block_count, step_rows, col_block),
        ),
    )
    chosen = chosen.reshape(row_block, slot_count)
    kernel_part = jnp.where(inside, 1.0 / (1.0 + chosen / (LAGS * FEATURES)), 0.0)
    slot_kernel = lax.psum(kernel_part, "col")
    mass = jnp.sum(slot_kernel, axis=1)
    markov = slot_kernel / mass[:, None]
    snap_positions = jnp.arange(snap_count, dtype=jnp.int32)

    def operator_block(pair):
        ids, weights = pair
        match = ids[:, :, None] == snap_positions[None, None, :]
        return jnp.sum(jnp.where(match, weights[:, :, None], 0.0), axis=1)

    transition = lax.map(
        operator_block,
        (
            neighbours.reshape(block_count, step_rows, slot_count),
            markov.reshape(block_count, step_rows, slot_count),
        ),
    )
    transition = transition.reshape(row_block, snap_count)
    piece_width = snap_count // (row_count * col_count)

    def apply_rows(basis_rows):
        return lax.dot_general(
            basis_rows,
            transition,
            (((1,), (1,)), ((), ())),
            precision=lax.Precision.HIGHEST,
            preferred_element_type=jnp.float32,
        )

    def own_piece(image):
        return lax.dynamic_slice_in_dim(image, col_at * piece_width, piece_width, 1)

    basis = start_basis
    for step in range(ITERS):
        piece = own_piece(apply_rows(basis))
        partial_gram = jnp.dot(
            piece, piece.T, precision=lax.Precision.HIGHEST, preferred_element_type=jnp.float32
        )
        gram_small = global_sum(partial_gram) / snap_count
        lower = jnp.linalg.cholesky(gram_small)
        basis = collect(jax.scipy.linalg.solve_triangular(lower, piece, lower=True))
    image_piece = own_piece(apply_rows(basis))
    basis_piece = lax.dynamic_slice_in_dim(
        basis, (row_at * col_count + col_at) * piece_width, piece_width, 1
    )
    partial_ray = jnp.dot(
        basis_piece,
        image_piece.T,
        precision=lax.Precision.HIGHEST,
        preferred_element_type=jnp.float32,
    )
    rayleigh = global_sum(partial_ray) / snap_count
    basis_rows = lax.dynamic_slice_in_dim(basis, row_start, row_block, 1)
    return (basis_rows, rayleigh)


def solution(mesh):
    placed = (P("row", "col"), P("row", None), P())
    return jax.shard_map(
        shards, mesh=mesh, in_specs=placed, out_specs=(P(None, "row"), P()), check_vma=False
    )
```

profile of v0, /device:TPU:1, one launch (start us, length us, event | category | flops | bytes accessed | tf_op | source)
XLA Modules:
  0.0 1007.9 jit_solution(16402256858035387622)
XLA Ops:
  8.0 90.6 %all-gather.2.cloned.1.call-done = bf16[4096,2048]{1,0:T(8,128)(2,1)} async-done(((bf16[512,2048]{1,0:T(8,128)(2,1)}), bf16[4096,2048]{1,0:T(8,128)(2,1)}) %all-gather.2.cloned.1.call-update) | async-done | bytes 16777232 | tf_op jit(solution)/shard_map/all_gather | solution.py:26
  108.7 21.4 %fusion.5 = bf16[16,320,2048]{2,1,0:T(8,128)(2,1)} fusion(bf16[15,64,2048]{2,1,0:T(8,128)(2,1)S(1)} %slice.69, bf16[16,256,2048]{2,1,0:T(8,128)(2,1)} %bitcast.64), kind=kLoop, calls=%fused_computation.15 | loop fusion | flops 62914560 | bytes 41680896 | tf_op jit(solution)/shard_map/concatenate | solution.py:44
  130.2 23.8 %select_convert_fusion = bf16[5120,576]{1,0:T(8,128)(2,1)} fusion(bf16[5120,2048]{1,0:T(8,128)(2,1)} %bitcast.70, f32[576]{0:T(1024)S(1)} %pad_dynamic-slice_fusion.2, f32[5120]{0:T(1024)S(1)} %add.130, pred[576]{0:T(1024)(128)(4,1)S(1)} %add_compare_fusion, pred[5120]{0:T(1024)(128)(4,1)S(1)} %fusion.17, s32[]{:T(128)S(6)} %select_n.56, ...), kind=kOutput, calls=%fused_computation.17 | convolution fusion | flops 12097290240 | bytes 43675460 | tf_op jit(solution)/shard_map/dot_general | solution.py:52
  154.1 80.7 %reduce-scatter.2.cloned.1.call-done = bf16[320,576]{1,0:T(8,128)(2,1)} async-done(((bf16[5120,576]{1,0:T(8,128)(2,1)}), bf16[320,576]{1,0:T(8,128)(2,1)}) %reduce-scatter.2.cloned.1.call-update) | async-done | bytes 368656 | tf_op jit(solution)/shard_map/reduce_scatter | solution.py:57
  238.1 28.1 %while.22 = (s32[]{:T(128)}, f32[32,16,128]{2,1,0:T(8,128)S(1)}, s32[32,16,128]{2,1,0:T(8,128)S(1)}, f32[32,16,256]{2,1,0:T(8,128)S(1)}, s32[]{:T(128)}) while((s32[]{:T(128)}, f32[32,16,128]{2,1,0:T(8,128)S(1)}, s32[32,16,128]{2,1,0:T(8,128)S(1)}, f32[32,16,256]{2,1,0:T(8,128)S(1)}, s32[]{:T(128)}) %tuple.63), condition=%wide.region_4.5_spmd.clone, body=%wide.region_2.4_spmd.clone.sunk | while | flops 1570818 | bytes 98377 | solution.py:77
  267.0 83.3 %all-reduce.6.cloned.1.call-done = f32[512,128]{1,0:T(8,128)} async-done(((f32[512,128]{1,0:T(8,128)}), f32[512,128]{1,0:T(8,128)}) %all-reduce.6.cloned.1.call-update) | async-done | bytes 262160 | tf_op jit(solution)/shard_map/psum | solution.py:86
  352.5 280.2 %while.23 = (s32[]{:T(128)}, f32[32,16,4096]{2,1,0:T(8,128)}, s32[32,16,128]{2,1,0:T(8,128)S(1)}, f32[32,16,128]{2,1,0:T(8,128)S(1)}, s32[]{:T(128)}) while((s32[]{:T(128)}, f32[32,16,4096]{2,1,0:T(8,128)}, s32[32,16,128]{2,1,0:T(8,128)S(1)}, f32[32,16,128]{2,1,0:T(8,128)S(1)}, s32[]{:T(128)}) %tuple.64), condition=%wide.region_9.10_spmd.clone, body=%wide.region_7.9_spmd.clone.sunk | while | flops 25100288 | bytes 836165 | solution.py:96
  361.3 8.0 select_reduce_fusion.6
  370.0 8.0 select_reduce_fusion.6
  378.8 8.0 select_reduce_fusion.6
  387.5 8.0 select_reduce_fusion.6
  396.3 8.0 select_reduce_fusion.6
  405.1 8.0 select_reduce_fusion.6
  413.8 8.0 select_reduce_fusion.6
  422.6 8.0 select_reduce_fusion.6
  431.4 8.0 select_reduce_fusion.6
  632.7 9.2 fusion.46
  642.1 65.8 %psum.29 = f32[32,32]{0,1:T(8,128)S(1)} all-reduce(f32[32,32]{0,1:T(8,128)S(1)} %fusion.36), channel_id=1, replica_groups=mesh['row'=8,'col'=16] {'row','col'}, use_global_device_ids=true, to_apply=%region_10.11 | all-reduce | flops 1024 | bytes 8192 | tf_op jit(solution)/shard_map/psum | solution.py:13
  714.8 63.7 %all_gather.10 = f32[32,4096]{0,1:T(8,128)S(1)} all-gather(f32[32,32]{0,1:T(8,128)S(1)} %fusion.23), channel_id=1, replica_groups=mesh['row'=8,'col'=16] {'row','col'}, dimensions={1}, use_global_device_ids=true | all-gather | bytes 528384 | tf_op jit(solution)/shard_map/all_gather | solution.py:17
  778.6 9.3 fusion.47
  788.1 65.0 %psum.30 = f32[32,32]{0,1:T(8,128)S(1)} all-reduce(f32[32,32]{0,1:T(8,128)S(1)} %fusion.33), channel_id=1, replica_groups=mesh['row'=8,'col'=16] {'row','col'}, use_global_device_ids=true, to_apply=%region_13.16 | all-reduce | flops 1024 | bytes 8192 | tf_op jit(solution)/shard_map/psum | solution.py:13
  860.2 65.1 %all_gather.11 = f32[32,4096]{0,1:T(8,128)S(1)} all-gather(f32[32,32]{0,1:T(8,128)S(1)} %fusion.20), channel_id=1, replica_groups=mesh['row'=8,'col'=16] {'row','col'}, dimensions={1}, use_global_device_ids=true | all-gather | bytes 528384 | tf_op jit(solution)/shard_map/all_gather | solution.py:17
  925.3 9.2 fusion.48
  934.8 65.0 %psum.31 = f32[32,32]{0,1:T(8,128)S(1)} all-reduce(f32[32,32]{0,1:T(8,128)S(1)} %fusion.29), channel_id=1, replica_groups=mesh['row'=8,'col'=16] {'row','col'}, use_global_device_ids=true, to_apply=%region_14.17 | all-reduce | flops 1024 | bytes 8192 | tf_op jit(solution)/shard_map/psum | solution.py:13
  (316 shorter events, 267.2 us)
Async XLA Ops:
  7.2 625.5 %copy-start = (f32[32,4096]{1,0:T(8,128)S(1)}, f32[32,4096]{1,0:T(8,128)}, u32[]{:S(2)}) copy-start(f32[32,4096]{1,0:T(8,128)} %param.12) | copy-start | bytes 1572868
  7.2 91.4 %all-gather.2.cloned.1.call-start = ((), (), s32[]{:S(2)}) async-start(), calls=%async_computation.1 | async-start | bytes 18874368 | tf_op jit(solution)/shard_map/all_gather | solution.py:26
  7.9 226.8 %reduce-scatter.2.cloned.1.call-start = ((), (), s32[]{:S(2)}) async-start(), calls=%async_computation.2 | async-start | bytes 6963200 | tf_op jit(solution)/shard_map/reduce_scatter | solution.py:57
  106.1 24.0 %slice-start = ((s8[16777216]{0:T(1024)(128)(4,1)}), s8[4194304]{0:T(1024)(128)(4,1)S(1)}, s32[]{:S(2)}) async-start(s8[16777216]{0:T(1024)(128)(4,1)} %bitcast.65), calls=%async_computation.4 | async-start | bytes 8388608
  108.7 21.5 %slice-start.1 = ((s8[16777216]{0:T(1024)(128)(4,1)}), s8[4194304]{0:T(1024)(128)(4,1)S(1)}, s32[]{:S(2)}) async-start(s8[16777216]{0:T(1024)(128)(4,1)} %bitcast.65), calls=%async_computation.5 | async-start | bytes 8388608
  108.7 21.4 %slice-start.2 = ((s8[16777216]{0:T(1024)(128)(4,1)}), s8[4194304]{0:T(1024)(128)(4,1)S(1)}, s32[]{:S(2)}) async-start(s8[16777216]{0:T(1024)(128)(4,1)} %bitcast.65), calls=%async_computation.6 | async-start | bytes 8388608
  108.7 21.4 %slice-start.3 = ((s8[16777216]{0:T(1024)(128)(4,1)}), s8[4194304]{0:T(1024)(128)(4,1)S(1)}, s32[]{:S(2)}) async-start(s8[16777216]{0:T(1024)(128)(4,1)} %bitcast.65), calls=%async_computation.7 | async-start | bytes 8388608
  130.1 23.9 %copy-start.1 = (s32[512,128]{1,0:T(8,128)S(1)}, s32[512,128]{1,0:T(8,128)}, u32[]{:S(2)}) copy-start(s32[512,128]{1,0:T(8,128)} %param.11) | copy-start | bytes 786436
  154.0 196.3 %all-reduce.6.cloned.1.call-start = ((), (), s32[]{:S(2)}) async-start(), calls=%async_computation.3 | async-start | bytes 524288 | tf_op jit(solution)/shard_map/psum | solution.py:86
Sparse Core Ops, SparseCore 0:
  9.7 88.8 all-gather.1
  154.1 80.6 reduce-scatter.1
  267.1 83.1 all-reduce.5
where the time goes:
time: 1020 us; the launch traced here: 1010 us
  other arithmetic  330 us (32%)
  blocking collectives  325 us (32%)
  waiting for transfers between devices  255 us (25%)
  matrix products  52.6 us (5%)
  local copies, waits for them, and re-layouts  29.2 us (3%)
  between operations  14.3 us (1%)
    reduce_sum x32, other arithmetic, operator_block(): return jnp.sum(jnp.where(match, weights[:, :, None], 0.0), axis=1)  256 us
    psum x3, blocking collectives, global_sum(): return lax.psum(value, ('row', 'col'))  196 us
    all_gather x2, blocking collectives, collect(): return lax.all_gather(columns, ('row', 'col'), axis=1, tiled=True)  129 us
    all_gather x1, waiting for transfers between devices, shards(): whole = lax.all_gather(snapshots, 'row', axis=0, tiled=True)  90.6 us
    psum x1, waiting for transfers between devices, shards(): slot_kernel = lax.psum(kernel_part, 'col')  83.3 us
    reduce_scatter x1, waiting for transfers between devices, shards(): lax.psum_scatter(jnp.where(keep, term, 0.0).astype(jnp.bfloat16), 'col',...  80.7 us
    dot_general x3, matrix products, apply_rows(): lax.dot_general(basis_rows, transition, (((1,), (1,)), ((), ())), precisi...  27.6 us
    reduce_sum x32, other arithmetic, pick_block(): return jnp.sum(jnp.where(match, lag_rows[:, None, :], 0.0), axis=2)  25.3 us
  transfers between devices with their start and end apart: 3, of which 3 were waited for; matrix products, arithmetic and copies ran while one was open for 0% of the time, Pallas kernels for 0%

commit v1 on v0

--- a/solution.py
+++ b/solution.py
@@ -83,7 +83,7 @@
     )
     chosen = chosen.reshape(row_block, slot_count)
     kernel_part = jnp.where(inside, 1.0 / (1.0 + chosen / (LAGS * FEATURES)), 0.0)
-    slot_kernel = lax.psum(kernel_part, "col")
+    slot_kernel = jnp.sum(lax.all_gather(kernel_part, "col"), axis=0)
     mass = jnp.sum(slot_kernel, axis=1)
     markov = slot_kernel / mass[:, None]
     snap_positions = jnp.arange(snap_count, dtype=jnp.int32)

time: 1020 us -> 986 us (0.967)
  waiting for transfers between devices: 255 us -> 224 us
    psum x1 -> x0, waiting for transfers between devices: 83.3 us -> none  [shards(): slot_kernel = lax.psum(kernel_part, 'col')]
    all_gather x0 -> x1, waiting for transfers between devices: none -> 52 us  [shards(): slot_kernel = jnp.sum(lax.all_gather(kernel_part, 'col'), axis=0)]
where the time goes in v1:
time: 986 us; the launch traced here: 979 us
  other arithmetic  333 us (34%)
  blocking collectives  324 us (33%)
  waiting for transfers between devices  224 us (23%)
  matrix products  52.3 us (5%)
  local copies, waits for them, and re-layouts  29.3 us (3%)
  between operations  14.3 us (1%)
    reduce_sum x32, other arithmetic, operator_block(): return jnp.sum(jnp.where(match, weights[:, :, None], 0.0), axis=1)  256 us
    psum x3, blocking collectives, global_sum(): return lax.psum(value, ('row', 'col'))  195 us
    all_gather x2, blocking collectives, collect(): return lax.all_gather(columns, ('row', 'col'), axis=1, tiled=True)  129 us
    all_gather x1, waiting for transfers between devices, shards(): whole = lax.all_gather(snapshots, 'row', axis=0, tiled=True)  90.6 us
    reduce_scatter x1, waiting for transfers between devices, shards(): lax.psum_scatter(jnp.where(keep, term, 0.0).astype(jnp.bfloat16), 'col',...  80.3 us
    all_gather x1, waiting for transfers between devices, shards(): slot_kernel = jnp.sum(lax.all_gather(kernel_part, 'col'), axis=0)  52 us
    dot_general x3, matrix products, apply_rows(): lax.dot_general(basis_rows, transition, (((1,), (1,)), ((), ())), precisi...  27.4 us
    reduce_sum x32, other arithmetic, pick_block(): return jnp.sum(jnp.where(match, lag_rows[:, None, :], 0.0), axis=2)  25.3 us
  transfers between devices with their start and end apart: 3, of which 3 were waited for; matrix products, arithmetic and copies ran while one was open for 0% of the time, Pallas kernels for 0%

profile of v1, /device:TPU:1, one launch (start us, length us, event | category | flops | bytes accessed | tf_op | source)
XLA Modules:
  0.0 979.2 jit_solution(11435574498841345638)
XLA Ops:
  8.0 90.6 %all-gather.4.cloned.1.call-done = bf16[4096,2048]{1,0:T(8,128)(2,1)} async-done(((bf16[512,2048]{1,0:T(8,128)(2,1)}), bf16[4096,2048]{1,0:T(8,128)(2,1)}) %all-gather.4.cloned.1.call-update) | async-done | bytes 16777232 | tf_op jit(solution)/shard_map/all_gather | solution.py:26
  108.7 21.4 %fusion.5 = bf16[16,320,2048]{2,1,0:T(8,128)(2,1)} fusion(bf16[15,64,2048]{2,1,0:T(8,128)(2,1)S(1)} %slice.69, bf16[16,256,2048]{2,1,0:T(8,128)(2,1)} %bitcast.65), kind=kLoop, calls=%fused_computation.15 | loop fusion | flops 62914560 | bytes 41680896 | tf_op jit(solution)/shard_map/concatenate | solution.py:44
  130.2 23.8 %select_convert_fusion = bf16[5120,576]{1,0:T(8,128)(2,1)} fusion(bf16[5120,2048]{1,0:T(8,128)(2,1)} %bitcast.71, f32[576]{0:T(1024)S(1)} %pad_dynamic-slice_fusion.2, f32[5120]{0:T(1024)S(1)} %add.128, pred[576]{0:T(1024)(128)(4,1)S(1)} %add_compare_fusion, pred[5120]{0:T(1024)(128)(4,1)S(1)} %fusion.17, s32[]{:T(128)S(6)} %select_n.56, ...), kind=kOutput, calls=%fused_computation.17 | convolution fusion | flops 12097290240 | bytes 43675460 | tf_op jit(solution)/shard_map/dot_general | solution.py:52
  154.5 80.3 %reduce-scatter.2.cloned.1.call-done = bf16[320,576]{1,0:T(8,128)(2,1)} async-done(((bf16[5120,576]{1,0:T(8,128)(2,1)}), bf16[320,576]{1,0:T(8,128)(2,1)}) %reduce-scatter.2.cloned.1.call-update) | async-done | bytes 368656 | tf_op jit(solution)/shard_map/reduce_scatter | solution.py:57
  238.2 27.6 %while.22 = (s32[]{:T(128)}, f32[32,16,128]{2,1,0:T(8,128)S(1)}, s32[32,16,128]{2,1,0:T(8,128)S(1)}, f32[32,16,256]{2,1,0:T(8,128)S(1)}, s32[]{:T(128)}) while((s32[]{:T(128)}, f32[32,16,128]{2,1,0:T(8,128)S(1)}, s32[32,16,128]{2,1,0:T(8,128)S(1)}, f32[32,16,256]{2,1,0:T(8,128)S(1)}, s32[]{:T(128)}) %tuple.63), condition=%wide.region_4.5_spmd.clone, body=%wide.region_2.4_spmd.clone.sunk | while | flops 1570818 | bytes 98377 | solution.py:77
  266.7 52.0 %all-gather.6.cloned.1.call-done = f32[8192,128]{1,0:T(8,128)} async-done(((f32[512,128]{1,0:T(8,128)}), f32[8192,128]{1,0:T(8,128)}) %all-gather.6.cloned.1.call-update) | async-done | bytes 4194320 | tf_op jit(solution)/shard_map/all_gather | solution.py:86
  324.7 280.2 %while.23 = (s32[]{:T(128)}, f32[32,16,4096]{2,1,0:T(8,128)}, s32[32,16,128]{2,1,0:T(8,128)S(1)}, f32[32,16,128]{2,1,0:T(8,128)S(1)}, s32[]{:T(128)}) while((s32[]{:T(128)}, f32[32,16,4096]{2,1,0:T(8,128)}, s32[32,16,128]{2,1,0:T(8,128)S(1)}, f32[32,16,128]{2,1,0:T(8,128)S(1)}, s32[]{:T(128)}) %tuple.61), condition=%wide.region_9.10_spmd.clone, body=%wide.region_7.9_spmd.clone.sunk | while | flops 25100288 | bytes 836165 | solution.py:96
  333.4 8.0 select_reduce_fusion.6
  342.2 8.0 select_reduce_fusion.6
  350.9 8.0 select_reduce_fusion.6
  359.7 8.0 select_reduce_fusion.6
  368.5 8.0 select_reduce_fusion.6
  377.2 8.0 select_reduce_fusion.6
  386.0 8.0 select_reduce_fusion.6
  394.7 8.0 select_reduce_fusion.6
  403.5 8.0 select_reduce_fusion.6
  604.9 9.1 fusion.46
  614.2 64.9 %psum.21 = f32[32,32]{0,1:T(8,128)S(1)} all-reduce(f32[32,32]{0,1:T(8,128)S(1)} %fusion.36), channel_id=1, replica_groups=mesh['row'=8,'col'=16] {'row','col'}, use_global_device_ids=true, to_apply=%region_10.11 | all-reduce | flops 1024 | bytes 8192 | tf_op jit(solution)/shard_map/psum | solution.py:13
  686.0 65.1 %all_gather.18 = f32[32,4096]{0,1:T(8,128)S(1)} all-gather(f32[32,32]{0,1:T(8,128)S(1)} %fusion.23), channel_id=1, replica_groups=mesh['row'=8,'col'=16] {'row','col'}, dimensions={1}, use_global_device_ids=true | all-gather | bytes 528384 | tf_op jit(solution)/shard_map/all_gather | solution.py:17
  751.2 9.3 fusion.47
  760.7 65.2 %psum.22 = f32[32,32]{0,1:T(8,128)S(1)} all-reduce(f32[32,32]{0,1:T(8,128)S(1)} %fusion.33), channel_id=1, replica_groups=mesh['row'=8,'col'=16] {'row','col'}, use_global_device_ids=true, to_apply=%region_13.16 | all-reduce | flops 1024 | bytes 8192 | tf_op jit(solution)/shard_map/psum | solution.py:13
  833.0 63.8 %all_gather.19 = f32[32,4096]{0,1:T(8,128)S(1)} all-gather(f32[32,32]{0,1:T(8,128)S(1)} %fusion.20), channel_id=1, replica_groups=mesh['row'=8,'col'=16] {'row','col'}, dimensions={1}, use_global_device_ids=true | all-gather | bytes 528384 | tf_op jit(solution)/shard_map/all_gather | solution.py:17
  896.8 9.0 fusion.48
  906.0 65.0 %psum.23 = f32[32,32]{0,1:T(8,128)S(1)} all-reduce(f32[32,32]{0,1:T(8,128)S(1)} %fusion.29), channel_id=1, replica_groups=mesh['row'=8,'col'=16] {'row','col'}, use_global_device_ids=true, to_apply=%region_14.17 | all-reduce | flops 1024 | bytes 8192 | tf_op jit(solution)/shard_map/psum | solution.py:13
  (320 shorter events, 271.5 us)
Async XLA Ops:
  7.2 597.7 %copy-start = (f32[32,4096]{1,0:T(8,128)S(1)}, f32[32,4096]{1,0:T(8,128)}, u32[]{:S(2)}) copy-start(f32[32,4096]{1,0:T(8,128)} %param.12) | copy-start | bytes 1572868
  7.2 91.4 %all-gather.4.cloned.1.call-start = ((), (), s32[]{:S(2)}) async-start(), calls=%async_computation.1 | async-start | bytes 18874368 | tf_op jit(solution)/shard_map/all_gather | solution.py:26
  7.9 226.9 %reduce-scatter.2.cloned.1.call-start = ((), (), s32[]{:S(2)}) async-start(), calls=%async_computation.2 | async-start | bytes 6963200 | tf_op jit(solution)/shard_map/reduce_scatter | solution.py:57
  106.1 24.0 %slice-start = ((s8[16777216]{0:T(1024)(128)(4,1)}), s8[4194304]{0:T(1024)(128)(4,1)S(1)}, s32[]{:S(2)}) async-start(s8[16777216]{0:T(1024)(128)(4,1)} %bitcast.66), calls=%async_computation.4 | async-start | bytes 8388608
  108.7 21.5 %slice-start.1 = ((s8[16777216]{0:T(1024)(128)(4,1)}), s8[4194304]{0:T(1024)(128)(4,1)S(1)}, s32[]{:S(2)}) async-start(s8[16777216]{0:T(1024)(128)(4,1)} %bitcast.66), calls=%async_computation.5 | async-start | bytes 8388608
  108.7 21.4 %slice-start.2 = ((s8[16777216]{0:T(1024)(128)(4,1)}), s8[4194304]{0:T(1024)(128)(4,1)S(1)}, s32[]{:S(2)}) async-start(s8[16777216]{0:T(1024)(128)(4,1)} %bitcast.66), calls=%async_computation.6 | async-start | bytes 8388608
  108.7 21.4 %slice-start.3 = ((s8[16777216]{0:T(1024)(128)(4,1)}), s8[4194304]{0:T(1024)(128)(4,1)S(1)}, s32[]{:S(2)}) async-start(s8[16777216]{0:T(1024)(128)(4,1)} %bitcast.66), calls=%async_computation.7 | async-start | bytes 8388608
  130.1 24.3 %copy-start.1 = (s32[512,128]{1,0:T(8,128)S(1)}, s32[512,128]{1,0:T(8,128)}, u32[]{:S(2)}) copy-start(s32[512,128]{1,0:T(8,128)} %param.11) | copy-start | bytes 786436
  154.0 164.7 %all-gather.6.cloned.1.call-start = ((), (), s32[]{:S(2)}) async-start(), calls=%async_computation.3 | async-start | bytes 4456448 | tf_op jit(solution)/shard_map/all_gather | solution.py:86
Sparse Core Ops, SparseCore 0:
  9.7 88.8 all-gather.3
  154.1 80.7 reduce-scatter.1
  266.8 51.8 all-gather.5
